TPU v7x, 256 devices: a whole 4x4x8 slice. The times are simulated.
256 devices in a mesh: req: 16 (over y, x), kv: 8 (over z), blk: 2 (over core).
Axes of the slice: x: 4, y: 4, z: 8, core: 2. Of those that a mesh axis runs over, the one named last changes fastest.
Arguments:
- x_resid: bfloat16 [16, 256, 5120], P('req', ('kv', 'blk')), may hold values from -54 to 54
- q_new: bfloat16 [16, 256, 4096], P('req', None, 'kv'), may hold values from -36 to 36
- k_new: bfloat16 [16, 256, 1024], P('req', None, 'kv'), may hold values from -6 to 12
- v_new: bfloat16 [16, 256, 1024], P('req', None, 'kv'), may hold values from -24 to 24
- k_cache: bfloat16 [16, 8, 64, 128, 128], P('req', 'kv', 'blk'), may hold values from -6 to 12
- v_cache: bfloat16 [16, 8, 64, 128, 128], P('req', 'kv', 'blk'), may hold values from -24 to 24
- cache_len: int32 [16], P('req'), may hold values from 1 to 7936, as said below
- page_table: int32 [16, 64], P('req'), may hold values from 0 to 63, as said below
- wo: bfloat16 [4096, 5120], P(('kv', 'blk')), may hold values from -0.09375 to 0.09375
- norm_gain: bfloat16 [5120], replicated, may hold values from 0.099609375 to 1.8984375
- w_gate: bfloat16 [5120, 7168], P('req', ('kv', 'blk')), may hold values from -0.078125 to 0.078125
- w_up: bfloat16 [5120, 7168], P('req', ('kv', 'blk')), may hold values from -0.078125 to 0.078125
- w_down: bfloat16 [7168, 5120], P(('kv', 'blk'), 'req'), may hold values from -0.0625 to 0.0625
Outputs:
- layer_out: bfloat16 [16, 256, 5120], P('req', ('kv', 'blk'))
- k_cache_out: bfloat16 [16, 8, 64, 128, 128], P('req', 'kv', 'blk')
- v_cache_out: bfloat16 [16, 8, 64, 128, 128], P('req', 'kv', 'blk')
Inputs may be any that keep to these rules, and one draw needn't show every extreme that they name: `cache_len`: at least one request has the largest length. `page_table`: each row is a permutation of 0 to 63.
All inputs are finite; a program needn't handle non-finite values.
Results may differ from a plain program's by a relative error of at most 0.0095.
Values may be sent and summed in bfloat16 or wider, within the bound.
A program may use at most 128 MiB of HBM per device.

v0:
```python
import math
import jax
import jax.numpy as jnp
from jax import lax
from jax.sharding import PartitionSpec as P


def combined_all(part, axis, combine):
    gathered = jax.tree.map(lambda a: lax.all_gather(a, axis), part)

    def take(source):
        return jax.tree.map(lambda a: lax.dynamic_index_in_dim(a, source, 0, False), gathered)

    return lax.fori_loop(
        1, lax.axis_size(axis), lambda source, state: combine(state, take(source)), take(0)
    )


def rotate(field, positions):
    half_width = field.shape[-1] // 2
    pair_index = jnp.arange(half_width, dtype=jnp.float32)
    frequency = jnp.power(1000000.0, -2.0 * pair_index / field.shape[-1])
    angles = positions.astype(jnp.float32)[:, None] * frequency[None, :]
    cosine = jnp.cos(angles)
    sine_part = jnp.sin(angles)
    lower_half = field[..., :half_width]
    upper_half = field[..., half_width:]
    return jnp.concatenate(
        [
            lower_half * cosine - upper_half * sine_part,
            upper_half * cosine + lower_half * sine_part,
        ],
        axis=-1,
    )


def merge_parts(first_part, second_part):
    max_first, total_first, out_first = first_part
    max_second, total_second, out_second = second_part
    overall = jnp.maximum(max_first, max_second)
    factor_first = jnp.exp(max_first - overall)
    factor_second = jnp.exp(max_second - overall)
    return (
        overall,
        factor_first * total_first + factor_second * total_second,
        factor_first[..., None] * out_first + factor_second[..., None] * out_second,
    )


def fetch_down(w_down):
    return lax.all_gather(w_down, "req", axis=1, tiled=True)


def rms_rows(rows, norm_gain):
    return (
        rows
        * lax.rsqrt(jnp.mean(rows * rows, axis=-1, keepdims=True) + 1e-05)
        * norm_gain.astype(jnp.float32)
    ).astype(jnp.bfloat16)


def on_device(
    x_resid,
    q_new,
    k_new,
    v_new,
    k_cache,
    v_cache,
    cache_len,
    page_table,
    wo,
    norm_gain,
    w_gate,
    w_up,
    w_down,
):
    blk_count = lax.axis_size("blk")
    blk_id = lax.axis_index("blk")
    new_tokens = q_new.shape[1]
    head_dim = k_new.shape[2]
    group_size = q_new.shape[2] // head_dim
    slot_count = k_cache.shape[2]
    page_size = k_cache.shape[3]
    page_total = page_table.shape[1]
    length = cache_len[0]
    positions = length + jnp.arange(new_tokens, dtype=jnp.int32)
    query_heads = rotate(
        q_new[0].reshape(new_tokens, group_size, head_dim).astype(jnp.float32).transpose(1, 0, 2),
        positions,
    ).astype(jnp.bfloat16)
    fresh_keys = rotate(k_new[0].astype(jnp.float32), positions).astype(jnp.bfloat16)
    page_ids = jnp.arange(page_total, dtype=jnp.int32)
    physical = blk_id * slot_count + jnp.arange(slot_count, dtype=jnp.int32)
    logical = jnp.sum(
        jnp.where(page_table[0][None, :] == physical[:, None], page_ids[None, :], 0), axis=1
    )
    slot_position = (
        logical[:, None] * page_size + jnp.arange(page_size, dtype=jnp.int32)[None, :]
    ).reshape(slot_count * page_size)
    new_index = slot_position - length
    is_new = (new_index >= 0) & (new_index < new_tokens)
    chosen = jnp.clip(new_index, 0, new_tokens - 1)
    key_rows = jnp.where(
        is_new[:, None], fresh_keys[chosen], k_cache[0, 0].reshape(slot_count * page_size, head_dim)
    )
    value_rows = jnp.where(
        is_new[:, None], v_new[0][chosen], v_cache[0, 0].reshape(slot_count * page_size, head_dim)
    )
    scores = jnp.einsum(
        "qd,sd->qs",
        query_heads.reshape(group_size * new_tokens, head_dim),
        key_rows,
        preferred_element_type=jnp.float32,
    ) * (1.0 / math.sqrt(head_dim))
    scores = scores.reshape(group_size, new_tokens, slot_count * page_size)
    allowed = slot_position[None, None, :] <= positions[None, :, None]
    masked = jnp.where(allowed, scores, -1e30)
    block_max = jnp.max(masked, axis=-1)
    weights = jnp.where(allowed, jnp.exp(masked - block_max[..., None]), 0.0).astype(jnp.bfloat16)
    block_total = jnp.sum(weights.astype(jnp.float32), axis=-1)
    block_out = jnp.einsum("gcs,sd->gcd", weights, value_rows, preferred_element_type=jnp.float32)
    merged = combined_all((block_max, block_total, block_out), "blk", merge_parts)
    attn = (merged[2] / merged[1][..., None]).astype(jnp.bfloat16)
    per_core = group_size // blk_count
    mine = lax.dynamic_slice_in_dim(attn, blk_id * per_core, per_core, 0)
    mine_rows = mine.transpose(1, 0, 2).reshape(new_tokens, per_core * head_dim)
    token_rows = x_resid.shape[1]
    row_start = lax.axis_index(("kv", "blk")) * token_rows
    partial_value = jnp.dot(mine_rows, wo, preferred_element_type=jnp.float32)
    own_part = lax.dynamic_slice_in_dim(partial_value, row_start, token_rows, 0) + x_resid[
        0
    ].astype(jnp.float32)
    contrib = lax.dynamic_update_slice_in_dim(partial_value, own_part, row_start, 0)
    resid = lax.psum(contrib, ("kv", "blk"))
    normed = rms_rows(resid, norm_gain)
    own_resid = lax.dynamic_slice_in_dim(resid, row_start, token_rows, 0)
    gate_val = jnp.dot(
        normed,
        lax.all_gather(w_gate, "req", axis=0, tiled=True),
        preferred_element_type=jnp.float32,
    )
    up_val = jnp.dot(
        normed, lax.all_gather(w_up, "req", axis=0, tiled=True), preferred_element_type=jnp.float32
    )
    hidden = (jax.nn.silu(gate_val) * up_val).astype(jnp.bfloat16)
    down_full = fetch_down(w_down)
    mlp_rows = lax.psum_scatter(
        jnp.dot(hidden, down_full, preferred_element_type=jnp.float32).astype(jnp.bfloat16),
        ("kv", "blk"),
        scatter_dimension=0,
        tiled=True,
    ).astype(jnp.float32)
    layer_out = (own_resid + mlp_rows).astype(jnp.bfloat16)[None]
    return (layer_out, key_rows.reshape(k_cache.shape), value_rows.reshape(v_cache.shape))


def solution(mesh):
    in_specs = (
        P("req", ("kv", "blk"), None),
        P("req", None, "kv"),
        P("req", None, "kv"),
        P("req", None, "kv"),
        P("req", "kv", "blk", None, None),
        P("req", "kv", "blk", None, None),
        P("req"),
        P("req", None),
        P(("kv", "blk"), None),
        P(),
        P("req", ("kv", "blk")),
        P("req", ("kv", "blk")),
        P(("kv", "blk"), "req"),
    )
    out_specs = (
        P("req", ("kv", "blk"), None),
        P("req", "kv", "blk", None, None),
        P("req", "kv", "blk", None, None),
    )
    return jax.shard_map(
        on_device, mesh=mesh, in_specs=in_specs, out_specs=out_specs, check_vma=False
    )
```

profile of v0, /device:TPU:2, one launch (start us, length us, event | category | flops | bytes accessed | tf_op | source)
XLA Modules:
  0.0 365.1 jit_solution(288112992523952814)
XLA Ops:
  11.4 1.9 reshape.295
  13.3 1.3 copy.30
  14.8 15.0 %gather_fusion = bf16[4096,128]{1,0:T(8,128)(2,1)} fusion(bf16[256,128]{1,0:T(8,128)(2,1)S(1)} %copy.32, s32[4096]{0:T(1024)S(1)} %broadcast_clamp_fusion), kind=kCustom, calls=%fused_computation | custom fusion | bytes 2113536 | tf_op jit(solution)/shard_map/gather | solution.py:104
  29.8 15.0 %gather_fusion.1 = bf16[4096,128]{1,0:T(8,128)(2,1)} fusion(bf16[256,128]{1,0:T(8,128)(2,1)S(1)} %bitcast.87, s32[4096]{0:T(1024)S(1)} %broadcast_clamp_fusion), kind=kCustom, calls=%fused_computation.1 | custom fusion | bytes 2113536 | tf_op jit(solution)/shard_map/gather | solution.py:107
  45.6 3.6 bitcast_select_fusion.2
  49.2 3.7 %fusion.1 = (f32[1024]{0:T(1024)S(1)}, f32[1024,4096]{1,0:T(8,128)S(1)}) fusion(pred[256,4096]{1,0:T(8,128)(4,1)S(1)} %broadcast_compare_fusion, bf16[4096,128]{1,0:T(8,128)(2,1)S(1)} %bitcast_select_fusion.2, bf16[1024,64]{0,1:T(8,128)(2,1)S(1)} %bitcast.95, bf16[1024,64]{0,1:T(8,128)(2,1)S(1)} %bitcast.94), kind=kOutput, calls=%fused_computation.6 | convolution fusion | flops 1086848000 | bytes 19140608 | tf_op jit(solution)/shard_map/qd,sd->qs/dot_general | solution.py:109
  52.9 6.7 %convert_reduce_fusion = (f32[1024]{0:T(1024)S(1)}, bf16[1024,4096]{1,0:T(8,128)(2,1)S(1)}) fusion(f32[1024]{0:T(1024)S(1)} %get-tuple-element.46, f32[1024,4096]{1,0:T(8,128)S(1)} %get-tuple-element.47, pred[256,4096]{1,0:T(8,128)(4,1)S(1)} %broadcast_compare_fusion), kind=kLoop, calls=%fused_computation.5 | loop fusion | flops 29359104 | bytes 26222592 | tf_op jit(solution)/shard_map/reduce_sum | solution.py:120
  59.7 1.5 broadcast_select_fusion
  61.2 1.0 copy-done.6
  62.2 3.2 fusion.34
  65.4 1.8 all_gather.32
  67.3 2.0 all_gather.28
  69.3 13.5 %all-gather.12.cloned.1.call-done = f32[8,256,128]{2,1,0:T(8,128)} async-done(((f32[4,256,128]{2,1,0:T(8,128)}), f32[8,256,128]{2,1,0:T(8,128)}) %all-gather.12.cloned.1.call-update) | async-done | bytes 1048592 | tf_op jit(solution)/shard_map/all_gather | solution.py:9
  82.8 1.3 fusion.33
  85.1 1.0 divide_convert_fusion
  86.2 3.2 fusion.35
  89.4 1.7 fusion.8
  92.9 126.8 %all-reduce.2.cloned.1.call-done = f32[256,5120]{1,0:T(8,128)} async-done(((f32[256,5120]{1,0:T(8,128)}), f32[256,5120]{1,0:T(8,128)}) %all-reduce.2.cloned.1.call-update) | async-done | bytes 5242896 | tf_op jit(solution)/shard_map/psum | solution.py:134
  219.8 2.9 multiply_reduce_fusion
  222.7 6.2 %fusion.29 = f32[256,448]{0,1:T(8,128)S(1)} fusion(bf16[5120,448]{1,0:T(8,128)(2,1)} %all-gather.6.cloned.1.call-done, f32[256,5120]{1,0:T(8,128)} %all-reduce.2.cloned.1.call-done, f32[5120]{0:T(1024)S(1)} %convert_element_type.69, f32[256]{0:T(256)S(1)} %add_rsqrt_fusion), kind=kOutput, calls=%fused_computation.74 | convolution fusion | flops 1178337280 | bytes 10310656 | tf_op jit(solution)/shard_map/dot_general | solution.py:137
  228.9 53.8 %all-gather.8.cloned.1.call-done = bf16[5120,448]{1,0:T(8,128)(2,1)} async-done(((bf16[320,448]{1,0:T(8,128)(2,1)}), bf16[5120,448]{1,0:T(8,128)(2,1)}) %all-gather.8.cloned.1.call-update) | async-done | bytes 4587536 | tf_op jit(solution)/shard_map/all_gather | solution.py:143
  282.8 12.4 %convolution_convert_fusion = bf16[256,5120]{1,0:T(8,128)(2,1)} fusion(bf16[448,5120]{0,1:T(8,128)(2,1)} %all-gather.10.cloned.1.call-done, bf16[5120,448]{1,0:T(8,128)(2,1)} %all-gather.8.cloned.1.call-done, f32[256,448]{0,1:T(8,128)S(1)} %fusion.29, f32[256,5120]{1,0:T(8,128)} %all-reduce.2.cloned.1.call-done, f32[5120]{0:T(1024)S(1)} %convert_element_type.69, ...), kind=kOutput, calls=%fused_computation.7 | convolution fusion | flops 2354741248 | bytes 17519616 | tf_op jit(solution)/shard_map/dot_general | solution.py:148
  295.2 60.8 %reduce-scatter.2.cloned.1.call-done = bf16[16,5120]{1,0:T(8,128)(2,1)} async-done(((bf16[256,5120]{1,0:T(8,128)(2,1)}), bf16[16,5120]{1,0:T(8,128)(2,1)}) %reduce-scatter.2.cloned.1.call-update) | async-done | bytes 163856 | tf_op jit(solution)/shard_map/reduce_scatter | solution.py:147
  356.0 1.8 fusion.14
  (62 shorter events, 6.4 us)
Async XLA Ops:
  8.0 78.2 %copy-start = (bf16[256,5120]{1,0:T(8,128)(2,1)S(1)}, bf16[256,5120]{1,0:T(8,128)(2,1)}, u32[]{:S(2)}) copy-start(bf16[256,5120]{1,0:T(8,128)(2,1)} %param.21) | copy-start | bytes 7864324
  8.0 74.8 %all-gather.12.cloned.1.call-start = ((), (), s32[]{:S(2)}) async-start(), calls=%async_computation.6 | async-start | bytes 1572864 | tf_op jit(solution)/shard_map/all_gather | solution.py:9
  14.6 15.2 %copy-start.1 = (bf16[1,256,128]{2,1,0:T(8,128)(2,1)S(1)}, bf16[1,256,128]{2,1,0:T(8,128)(2,1)}, u32[]{:S(2)}) copy-start(bf16[1,256,128]{2,1,0:T(8,128)(2,1)} %param.16) | copy-start | bytes 196612
  52.9 6.8 %copy-start.2 = (bf16[4096,128]{1,0:T(8,128)(2,1)S(1)}, bf16[4096,128]{1,0:T(8,128)(2,1)}, u32[]{:S(2)}) copy-start(bf16[4096,128]{1,0:T(8,128)(2,1)} %gather_fusion) | copy-start | bytes 3145732
  52.9 6.8 %copy-start.3 = (bf16[4096,128]{1,0:T(8,128)(2,1)S(1)}, bf16[4096,128]{1,0:T(8,128)(2,1)}, u32[]{:S(2)}) copy-start(bf16[4096,128]{1,0:T(8,128)(2,1)} %gather_fusion.1) | copy-start | bytes 3145732
  52.9 6.8 %copy-start.4 = (bf16[1,1,32,128,128]{4,3,2,1,0:T(8,128)(2,1)S(1)}, bf16[1,1,32,128,128]{4,3,2,1,0:T(8,128)(2,1)}, u32[]{:S(2)}) copy-start(bf16[1,1,32,128,128]{4,3,2,1,0:T(8,128)(2,1)} %param.17) | copy-start | bytes 3145732
  52.9 6.8 %copy-start.5 = (bf16[1,1,32,128,128]{4,3,2,1,0:T(8,128)(2,1)S(1)}, bf16[1,1,32,128,128]{4,3,2,1,0:T(8,128)(2,1)}, u32[]{:S(2)}) copy-start(bf16[1,1,32,128,128]{4,3,2,1,0:T(8,128)(2,1)} %param.18) | copy-start | bytes 3145732
  61.2 1.0 copy-start.6
  65.4 154.4 %all-reduce.2.cloned.1.call-start = ((), (), s32[]{:S(2)}) async-start(), calls=%async_computation.1 | async-start | bytes 10485760 | tf_op jit(solution)/shard_map/psum | solution.py:134
  85.0 4.4 %copy-start.7 = (bf16[1,16,5120]{2,1,0:T(8,128)(2,1)S(1)}, bf16[1,16,5120]{2,1,0:T(8,128)(2,1)}, u32[]{:S(2)}) copy-start(bf16[1,16,5120]{2,1,0:T(8,128)(2,1)} %param.13) | copy-start | bytes 491524
  89.4 3.6 copy-start.8
  91.1 131.6 %all-gather.6.cloned.1.call-start = ((), (), s32[]{:S(2)}) async-start(), calls=%async_computation.2 | async-start | bytes 5570560 | tf_op jit(solution)/shard_map/all_gather | solution.py:139
  91.7 137.2 %all-gather.10.cloned.1.call-start = ((), (), s32[]{:S(2)}) async-start(), calls=%async_computation.4 | async-start | bytes 5570560 | tf_op jit(solution)/shard_map/all_gather | solution.py:51
  92.3 190.5 %all-gather.8.cloned.1.call-start = ((), (), s32[]{:S(2)}) async-start(), calls=%async_computation.3 | async-start | bytes 5570560 | tf_op jit(solution)/shard_map/all_gather | solution.py:143
  92.9 263.1 %reduce-scatter.2.cloned.1.call-start = ((), (), s32[]{:S(2)}) async-start(), calls=%async_computation.5 | async-start | bytes 2785280 | tf_op jit(solution)/shard_map/reduce_scatter | solution.py:147
Sparse Core Ops, SparseCore 0:
  65.5 17.2 all-gather.11
  91.2 128.4 all-reduce.1
  295.3 60.6 reduce-scatter.1
Sparse Core Ops, SparseCore 1:
  94.0 62.4 all-gather.5
  158.8 60.7 all-gather.9
  221.9 60.8 all-gather.7
where the time goes:
time: 365 us
  waiting for transfers between devices  257 us (70%)
  local copies, waits for them, and re-layouts  37.7 us (10%)
  matrix products  28.6 us (8%)
  other arithmetic  21.5 us (6%)
  between operations  16.6 us (5%)
  blocking collectives  3.81 us (1%)
    psum x1, waiting for transfers between devices, on_device(): resid = lax.psum(contrib, ('kv', 'blk'))  127 us
    reduce_scatter x1, waiting for transfers between devices, on_device(): lax.psum_scatter(jnp.dot(hidden, down_full, preferred_element_type=jnp.fl...  60.8 us
    all_gather x1, waiting for transfers between devices, on_device(): lax.all_gather(w_up, 'req', axis=0, tiled=True)  53.8 us
    gather x1, local copies, waits for them, and re-layouts, on_device(): fresh_keys[chosen]  15 us
    gather x1, local copies, waits for them, and re-layouts, on_device(): v_new[0][chosen]  15 us
    all_gather x1, waiting for transfers between devices, combined_all(): gathered = jax.tree.map(lambda a: lax.all_gather(a, axis), part)  13.5 us
    dot_general x1, matrix products, on_device(): jnp.dot(hidden, down_full, preferred_element_type=jnp.float32)  12.4 us
  transfers between devices with their start and end apart: 6, of which 4 were waited for; matrix products, arithmetic and copies ran while one was open for 2% of the time, Pallas kernels for 0%

commit v1 on v0

--- a/solution.py
+++ b/solution.py
@@ -139,9 +139,20 @@
         lax.all_gather(w_gate, "req", axis=0, tiled=True),
         preferred_element_type=jnp.float32,
     )
-    up_val = jnp.dot(
-        normed, lax.all_gather(w_up, "req", axis=0, tiled=True), preferred_element_type=jnp.float32
-    )
+
+    def answer_sides(block_in, in_dim):
+        extra = jnp.concatenate(
+            lax.all_to_all(
+                jnp.stack(lax.psum(1, axis_name="req") * [block_in], axis=0),
+                axis_name="req",
+                concat_axis=0,
+                split_axis=0,
+            ),
+            axis=in_dim,
+        )
+        return extra
+
+    up_val = jnp.dot(normed, answer_sides(w_up, 0), preferred_element_type=jnp.float32)
     hidden = (jax.nn.silu(gate_val) * up_val).astype(jnp.bfloat16)
     down_full = fetch_down(w_down)
     mlp_rows = lax.psum_scatter(

time: 365 us -> 352 us (0.964)
  waiting for transfers between devices: 257 us -> 232 us
  starting transfers between devices: 0.25 us -> 7.6 us
    all_gather x1 -> x0, waiting for transfers between devices: 53.8 us -> none  [on_device(): lax.all_gather(w_up, 'req', axis=0, tiled=True)]
    all_gather x1, waiting for transfers between devices: 0.03 us -> 38.7 us  [fetch_down(): return lax.all_gather(w_down, 'req', axis=1, tiled=True)]
    psum x1, waiting for transfers between devices: 127 us -> 118 us  [on_device(): resid = lax.psum(contrib, ('kv', 'blk'))]
    all_to_all x0 -> x1, starting transfers between devices: none -> 7.4 us  [answer_sides(): lax.all_to_all(jnp.stack(lax.psum(1, axis_name='req') * [block_in], axis=...]
  transfers between devices with their start and end apart: 6 -> 6, of which waited for: 4 -> 4; matrix products, arithmetic and copies ran while one was open for 2% -> 3% of each run, Pallas kernels for 0% -> 0%
where the time goes in v1:
time: 352 us; the launch traced here: 351 us
  waiting for transfers between devices  232 us (66%)
  local copies, waits for them, and re-layouts  40.5 us (12%)
  matrix products  28.9 us (8%)
  other arithmetic  21.6 us (6%)
  between operations  16.4 us (5%)
  starting transfers between devices  7.6 us (2%)
  blocking collectives  3.81 us (1%)
    psum x1, waiting for transfers between devices, on_device(): resid = lax.psum(contrib, ('kv', 'blk'))  118 us
    reduce_scatter x1, waiting for transfers between devices, on_device(): lax.psum_scatter(jnp.dot(hidden, down_full, preferred_element_type=jnp.fl...  60.8 us
    all_gather x1, waiting for transfers between devices, fetch_down(): return lax.all_gather(w_down, 'req', axis=1, tiled=True)  38.7 us
    gather x1, local copies, waits for them, and re-layouts, on_device(): fresh_keys[chosen]  15 us
    gather x1, local copies, waits for them, and re-layouts, on_device(): v_new[0][chosen]  15 us
    all_gather x1, waiting for transfers between devices, combined_all(): gathered = jax.tree.map(lambda a: lax.all_gather(a, axis), part)  13.5 us
    dot_general x1, matrix products, on_device(): jnp.dot(hidden, down_full, preferred_element_type=jnp.float32)  12.5 us
    all_to_all x1, starting transfers between devices, answer_sides(): lax.all_to_all(jnp.stack(lax.psum(1, axis_name='req') * [block_in], axis=...  7.4 us
  transfers between devices with their start and end apart: 6, of which 4 were waited for; matrix products, arithmetic and copies ran while one was open for 3% of the time, Pallas kernels for 0%

profile of v1, /device:TPU:2, one launch (start us, length us, event | category | flops | bytes accessed | tf_op | source)
XLA Modules:
  0.0 351.1 jit_solution(7333776123338255573)
XLA Ops:
  11.4 1.9 reshape.301
  13.3 1.3 copy.30
  14.8 15.0 %gather_fusion = bf16[4096,128]{1,0:T(8,128)(2,1)} fusion(bf16[256,128]{1,0:T(8,128)(2,1)S(1)} %copy.32, s32[4096]{0:T(1024)S(1)} %broadcast_clamp_fusion), kind=kCustom, calls=%fused_computation | custom fusion | bytes 2113536 | tf_op jit(solution)/shard_map/gather | solution.py:104
  29.8 15.0 %gather_fusion.1 = bf16[4096,128]{1,0:T(8,128)(2,1)} fusion(bf16[256,128]{1,0:T(8,128)(2,1)S(1)} %bitcast.88, s32[4096]{0:T(1024)S(1)} %broadcast_clamp_fusion), kind=kCustom, calls=%fused_computation.1 | custom fusion | bytes 2113536 | tf_op jit(solution)/shard_map/gather | solution.py:107
  45.6 3.6 %bitcast_select_fusion.2 = bf16[4096,128]{1,0:T(8,128)(2,1)S(1)} fusion(bf16[4096,128]{1,0:T(8,128)(2,1)} %gather_fusion, bf16[1,1,32,128,128]{4,3,2,1,0:T(8,128)(2,1)} %param.17, pred[4096]{0:T(1024)(128)(4,1)S(1)} %compare_and_fusion), kind=kLoop, calls=%fused_computation.13 | loop fusion | flops 524288 | bytes 3149824 | tf_op jit(solution)/shard_map/jit(_where)/select_n | solution.py:103
  49.2 3.7 %fusion.1 = (f32[1024]{0:T(1024)S(1)}, f32[1024,4096]{1,0:T(8,128)S(1)}) fusion(pred[256,4096]{1,0:T(8,128)(4,1)S(1)} %broadcast_compare_fusion, bf16[4096,128]{1,0:T(8,128)(2,1)S(1)} %bitcast_select_fusion.2, bf16[1024,64]{0,1:T(8,128)(2,1)S(1)} %bitcast.96, bf16[1024,64]{0,1:T(8,128)(2,1)S(1)} %bitcast.95), kind=kOutput, calls=%fused_computation.6 | convolution fusion | flops 1086848000 | bytes 19140608 | tf_op jit(solution)/shard_map/qd,sd->qs/dot_general | solution.py:109
  52.9 6.7 %convert_reduce_fusion = (f32[1024]{0:T(1024)S(1)}, bf16[1024,4096]{1,0:T(8,128)(2,1)S(1)}) fusion(f32[1024]{0:T(1024)S(1)} %get-tuple-element.46, f32[1024,4096]{1,0:T(8,128)S(1)} %get-tuple-element.47, pred[256,4096]{1,0:T(8,128)(4,1)S(1)} %broadcast_compare_fusion), kind=kLoop, calls=%fused_computation.5 | loop fusion | flops 29359104 | bytes 26222592 | tf_op jit(solution)/shard_map/reduce_sum | solution.py:120
  59.7 1.5 broadcast_select_fusion
  62.2 3.2 fusion.34
  65.4 1.8 all_gather.29
  67.3 2.0 all_gather.25
  69.3 13.5 %all-gather.9.cloned.1.call-done = f32[8,256,128]{2,1,0:T(8,128)} async-done(((f32[4,256,128]{2,1,0:T(8,128)}), f32[8,256,128]{2,1,0:T(8,128)}) %all-gather.9.cloned.1.call-update) | async-done | bytes 1048592 | tf_op jit(solution)/shard_map/all_gather | solution.py:9
  82.8 1.3 fusion.33
  86.1 3.3 fusion.35
  89.4 1.8 fusion.8
  92.4 2.8 stack.2
  95.2 7.4 %all-to-all-start = ((bf16[16,320,448]{2,1,0:T(8,128)(2,1)}), bf16[16,320,448]{2,1,0:T(8,128)(2,1)}, u32[]{:S(2)}, u32[]{:S(2)}) async-start(bf16[16,320,448]{2,1,0:T(8,128)(2,1)} %stack.2), calls=%async_computation | async-start | bytes 10485760 | tf_op jit(solution)/shard_map/all_to_all | solution.py:145
  102.7 118.1 %all-reduce.2.cloned.1.call-done = f32[256,5120]{1,0:T(8,128)} async-done(((f32[256,5120]{1,0:T(8,128)}), f32[256,5120]{1,0:T(8,128)}) %all-reduce.2.cloned.1.call-update) | async-done | bytes 5242896 | tf_op jit(solution)/shard_map/psum | solution.py:134
  220.8 3.0 multiply_reduce_fusion
  223.9 6.3 %fusion.29 = f32[256,448]{0,1:T(8,128)S(1)} fusion(bf16[5120,448]{1,0:T(8,128)(2,1)} %all-gather.5.cloned.1.call-done, f32[256,5120]{1,0:T(8,128)} %all-reduce.2.cloned.1.call-done, f32[5120]{0:T(1024)S(1)} %convert_element_type.69, f32[256]{0:T(256)S(1)} %add_rsqrt_fusion), kind=kOutput, calls=%fused_computation.74 | convolution fusion | flops 1178337280 | bytes 10310656 | tf_op jit(solution)/shard_map/dot_general | solution.py:137
  230.1 38.7 %all-gather.7.cloned.1.call-done = bf16[448,5120]{0,1:T(8,128)(2,1)} async-done(((bf16[448,320]{0,1:T(8,128)(2,1)}), bf16[448,5120]{0,1:T(8,128)(2,1)}) %all-gather.7.cloned.1.call-update) | async-done | bytes 4587536 | tf_op jit(solution)/shard_map/all_gather | solution.py:51
  268.9 12.5 %convolution_convert_fusion = bf16[256,5120]{1,0:T(8,128)(2,1)} fusion(bf16[448,5120]{0,1:T(8,128)(2,1)} %all-gather.7.cloned.1.call-done, bf16[5120,448]{1,0:T(8,128)(2,1)} %bitcast.22, f32[256,448]{0,1:T(8,128)S(1)} %fusion.29, f32[256,5120]{1,0:T(8,128)} %all-reduce.2.cloned.1.call-done, f32[5120]{0:T(1024)S(1)} %convert_element_type.69, ...), kind=kOutput, calls=%fused_computation.7 | convolution fusion | flops 2354741248 | bytes 17519616 | tf_op jit(solution)/shard_map/dot_general | solution.py:159
  281.4 60.8 %reduce-scatter.2.cloned.1.call-done = bf16[16,5120]{1,0:T(8,128)(2,1)} async-done(((bf16[256,5120]{1,0:T(8,128)(2,1)}), bf16[16,5120]{1,0:T(8,128)(2,1)}) %reduce-scatter.2.cloned.1.call-update) | async-done | bytes 163856 | tf_op jit(solution)/shard_map/reduce_scatter | solution.py:158
  342.3 1.8 fusion.14
  (66 shorter events, 7.8 us)
Async XLA Ops:
  8.0 78.1 %copy-start = (bf16[256,5120]{1,0:T(8,128)(2,1)S(1)}, bf16[256,5120]{1,0:T(8,128)(2,1)}, u32[]{:S(2)}) copy-start(bf16[256,5120]{1,0:T(8,128)(2,1)} %param.21) | copy-start | bytes 7864324
  8.0 74.8 %all-gather.9.cloned.1.call-start = ((), (), s32[]{:S(2)}) async-start(), calls=%async_computation.6 | async-start | bytes 1572864 | tf_op jit(solution)/shard_map/all_gather | solution.py:9
  14.6 15.2 %copy-start.2 = (bf16[1,256,128]{2,1,0:T(8,128)(2,1)S(1)}, bf16[1,256,128]{2,1,0:T(8,128)(2,1)}, u32[]{:S(2)}) copy-start(bf16[1,256,128]{2,1,0:T(8,128)(2,1)} %param.16) | copy-start | bytes 196612
  52.9 6.8 %copy-start.3 = (bf16[4096,128]{1,0:T(8,128)(2,1)S(1)}, bf16[4096,128]{1,0:T(8,128)(2,1)}, u32[]{:S(2)}) copy-start(bf16[4096,128]{1,0:T(8,128)(2,1)} %gather_fusion) | copy-start | bytes 3145732
  52.9 6.8 %copy-start.4 = (bf16[4096,128]{1,0:T(8,128)(2,1)S(1)}, bf16[4096,128]{1,0:T(8,128)(2,1)}, u32[]{:S(2)}) copy-start(bf16[4096,128]{1,0:T(8,128)(2,1)} %gather_fusion.1) | copy-start | bytes 3145732
  52.9 6.8 %copy-start.5 = (bf16[1,1,32,128,128]{4,3,2,1,0:T(8,128)(2,1)S(1)}, bf16[1,1,32,128,128]{4,3,2,1,0:T(8,128)(2,1)}, u32[]{:S(2)}) copy-start(bf16[1,1,32,128,128]{4,3,2,1,0:T(8,128)(2,1)} %param.17) | copy-start | bytes 3145732
  52.9 6.8 %copy-start.6 = (bf16[1,1,32,128,128]{4,3,2,1,0:T(8,128)(2,1)S(1)}, bf16[1,1,32,128,128]{4,3,2,1,0:T(8,128)(2,1)}, u32[]{:S(2)}) copy-start(bf16[1,1,32,128,128]{4,3,2,1,0:T(8,128)(2,1)} %param.18) | copy-start | bytes 3145732
  61.2 1.0 copy-start.7
  65.3 155.5 %all-reduce.2.cloned.1.call-start = ((), (), s32[]{:S(2)}) async-start(), calls=%async_computation.2 | async-start | bytes 10485760 | tf_op jit(solution)/shard_map/psum | solution.py:134
  85.0 4.4 %copy-start.9 = (bf16[1,16,5120]{2,1,0:T(8,128)(2,1)S(1)}, bf16[1,16,5120]{2,1,0:T(8,128)(2,1)}, u32[]{:S(2)}) copy-start(bf16[1,16,5120]{2,1,0:T(8,128)(2,1)} %param.13) | copy-start | bytes 491524
  89.4 3.0 copy-start.8
  91.2 132.6 %all-gather.5.cloned.1.call-start = ((), (), s32[]{:S(2)}) async-start(), calls=%async_computation.3 | async-start | bytes 5570560 | tf_op jit(solution)/shard_map/all_gather | solution.py:139
  91.8 177.1 %all-gather.7.cloned.1.call-start = ((), (), s32[]{:S(2)}) async-start(), calls=%async_computation.4 | async-start | bytes 5570560 | tf_op jit(solution)/shard_map/all_gather | solution.py:51
  95.2 7.5 %copy-start.10 = (bf16[5120]{0:T(1024)(128)(2,1)S(1)}, bf16[5120]{0:T(1024)(128)(2,1)}, u32[]{:S(2)}) copy-start(bf16[5120]{0:T(1024)(128)(2,1)} %param.22) | copy-start | bytes 30724
  95.2 134.9 %all-to-all-start = ((bf16[16,320,448]{2,1,0:T(8,128)(2,1)}), bf16[16,320,448]{2,1,0:T(8,128)(2,1)}, u32[]{:S(2)}, u32[]{:S(2)}) async-start(bf16[16,320,448]{2,1,0:T(8,128)(2,1)} %stack.2), calls=%async_computation | async-start | bytes 10485760 | tf_op jit(solution)/shard_map/all_to_all | solution.py:145
  102.6 239.6 %reduce-scatter.2.cloned.1.call-start = ((), (), s32[]{:S(2)}) async-start(), calls=%async_computation.5 | async-start | bytes 2785280 | tf_op jit(solution)/shard_map/reduce_scatter | solution.py:158
  268.9 75.1 %copy-start.1 = (bf16[256,5120]{1,0:T(8,128)(2,1)S(1)}, bf16[256,5120]{1,0:T(8,128)(2,1)}, u32[]{:S(2)}) copy-start(bf16[256,5120]{1,0:T(8,128)(2,1)} %param.21) | copy-start | bytes 7864324
Sparse Core Ops, SparseCore 0:
  65.5 17.2 all-gather.8
  91.3 129.4 all-reduce.1
  281.5 60.6 reduce-scatter.1
Sparse Core Ops, SparseCore 1:
  94.1 109.6 all-gather.4
  206.0 62.8 all-gather.6
